TPU v7x, 32 devices: a whole 2x2x4 slice. The times are simulated.
32 devices in a mesh: tile: 4 (over y, core), dp: 8 (over z, x).
Axes of the slice: x: 2, y: 2, z: 4, core: 2. Of those that a mesh axis runs over, the one named last changes fastest.
Arguments:
- observed: float32 [8, 2, 8, 32], P('dp', None, 'tile'), may hold values from -6 to 6
- targets: float32 [8, 2, 8, 32], P('dp', None, 'tile'), may hold values from -6 to 6
- pixel_mask: int32 [8, 2, 8, 32], P('dp', None, 'tile'), may hold values 0 or 1
- lengths: int32 [8], P('dp'), may hold values from 1 to 2, as said below
- step_count: int32 [1], replicated, may hold values from 2 to 20
- kernels: float32 [1, 12800, 1024], P(None, 'dp'), may hold values from -0.0546875 to 0.0546875
- kernel_moment: float32 [1, 12800, 1024], P(None, 'dp'), may hold values from -7.6293945e-06 to 7.6293945e-06
- kernel_second: float32 [1, 12800, 1024], P(None, 'dp'), may hold values from 1.9073486e-12 to 7.6293945e-12
- norm_params: float32 [2, 1, 1024], replicated
- norm_moment: float32 [2, 1, 1024], replicated, may hold values from -1.5258789e-05 to 1.5258789e-05
- norm_second: float32 [2, 1, 1024], replicated, may hold values from 7.6293945e-12 to 3.0517578e-11
- end_params: float32 [3, 256], replicated
- end_moment: float32 [3, 256], replicated, may hold values from -7.6293945e-05 to 7.6293945e-05
- end_second: float32 [3, 256], replicated, may hold values from 1.9073486e-10 to 7.6293943e-10
- head_bias: float32 [1], replicated, may hold values from -3 to 3
- head_moment: float32 [1], replicated, may hold values from -0.0546875 to 0.0546875
- head_second: float32 [1], replicated, may hold values from 7.6293945e-05 to 0.00030517578
- hidden_init: float32 [1, 8, 8, 32, 256], P(None, 'dp', 'tile'), may hold values from -0.9 to 0.9
- cells_init: float32 [1, 8, 8, 32, 256], P(None, 'dp', 'tile'), may hold values from -5 to 5
Outputs:
- loss_value: float32 [], replicated
- grad_norm: float32 [], replicated
- kernels_new: float32 [1, 12800, 1024], P(None, 'dp')
- kernel_moment_new: float32 [1, 12800, 1024], P(None, 'dp')
- kernel_second_new: float32 [1, 12800, 1024], P(None, 'dp')
- norm_new: float32 [2, 1, 1024], replicated
- norm_moment_new: float32 [2, 1, 1024], replicated
- norm_second_new: float32 [2, 1, 1024], replicated
- end_new: float32 [3, 256], replicated
- end_moment_new: float32 [3, 256], replicated
- end_second_new: float32 [3, 256], replicated
- head_new: float32 [1], replicated
- head_moment_new: float32 [1], replicated
- head_second_new: float32 [1], replicated
- hidden_final: float32 [1, 8, 8, 32, 256], P(None, 'dp', 'tile')
- cells_final: float32 [1, 8, 8, 32, 256], P(None, 'dp', 'tile')
Inputs may be any that keep to these rules, and one draw needn't show every extreme that they name: `lengths`: some stream has all 2 frames counting and some only one.
All inputs are finite; a program needn't handle non-finite values. No bound on the sum of `pixel_mask` on one device may be relied on, other than what follows from the above.
Results may differ from a plain program's by a relative error of at most 0.0003.
The roundings to bfloat16 on the way count: a program that leaves them out, or rounds other values in their place, can miss the bound.
Values may be sent and summed in bfloat16 or wider, within the bound.
No kernel may reach another device: no remote copies, remote signals or barrier semaphores. Data moves between devices by JAX's collectives and lax.ppermute only.
A program may use at most 192 MiB of HBM per device.

v0:
```python
import jax
import jax.numpy as jnp
from jax import lax
from jax.sharding import PartitionSpec as P

IN_DIM = 512
KERNEL = 5
GROUP_SIZE = 64
clip_limit = 0.005
small_rate = 0.1


def padded_2(cells, sides, width):
    for axis, dim in sides:
        count = lax.axis_size(axis)
        ends = count - 1
        head = lax.slice_in_dim(cells, 0, width, axis=dim)
        tail = lax.slice_in_dim(cells, cells.shape[dim] - width, cells.shape[dim], axis=dim)
        cells = jnp.concatenate(
            [
                lax.ppermute(tail, axis, [(i, (i + 1) % count) for i in range(ends)]),
                cells,
                lax.ppermute(head, axis, [((i + 1) % count, i) for i in range(ends)]),
            ],
            axis=dim,
        )
    return cells


def group_norm(gates, gain, shift):
    full_shape = gates.shape
    grouped = gates.reshape(full_shape[:-1] + (full_shape[-1] // GROUP_SIZE, GROUP_SIZE))
    centred = grouped - jnp.mean(grouped, axis=-1, keepdims=True)
    spread = jnp.mean(centred * centred, axis=-1, keepdims=True)
    return (centred * lax.rsqrt(spread + 1e-05)).reshape(full_shape) * gain + shift


def lstm_cell(gates, cells_prev, gain, shift):
    normed = group_norm(gates, gain, shift)
    quarter = normed.shape[-1] // 4
    input_gate = jax.nn.sigmoid(normed[..., :quarter])
    forget_gate = jax.nn.sigmoid(normed[..., quarter : 2 * quarter])
    candidate = jnp.tanh(normed[..., 2 * quarter : 3 * quarter])
    output_gate = jax.nn.sigmoid(normed[..., 3 * quarter :])
    cells_next = forget_gate * cells_prev + input_gate * candidate
    return (output_gate * jnp.tanh(cells_next), cells_next)


def unfold(padded, rows, columns):
    pieces = []
    for row_off in range(KERNEL):
        for col_off in range(KERNEL):
            pieces.append(padded[:, row_off : row_off + rows, col_off : col_off + columns, :])
    joined = jnp.concatenate(pieces, axis=-1)
    return joined.reshape(-1, joined.shape[-1])


def pad_columns(values):
    margin = KERNEL // 2
    return jnp.pad(values, ((0, 0), (0, 0), (margin, margin), (0, 0)))


def layer_forward(weight_full, gain, shift, inputs_low, hidden_start, cells_start):
    rows, columns = (hidden_start.shape[1], hidden_start.shape[2])
    hidden_low = hidden_start.astype(jnp.bfloat16)
    cells = cells_start
    kept = []
    outputs = []
    outputs_low = []
    hidden = hidden_start
    for frame_no in range(len(inputs_low)):
        joined = jnp.concatenate([inputs_low[frame_no], hidden_low], axis=-1)
        padded = padded_2(joined, (("tile", 1),), KERNEL // 2)
        padded = pad_columns(padded)
        gates = jnp.dot(
            unfold(padded, rows, columns), weight_full, preferred_element_type=jnp.float32
        )
        gates = gates.reshape(hidden_start.shape[:3] + (weight_full.shape[1],))
        kept.append((padded, gates, cells))
        hidden, cells = lstm_cell(gates, cells, gain, shift)
        hidden_low = hidden.astype(jnp.bfloat16)
        outputs.append(hidden)
        outputs_low.append(hidden_low)
    return (outputs, outputs_low, kept, hidden, cells)


def layer_backward(weight_full, gain, shift, kept, grad_above):
    pixel_shape = kept[0][1].shape
    rows, columns, gate_dim = (pixel_shape[1], pixel_shape[2], pixel_shape[3])
    in_dim = weight_full.shape[0] // (KERNEL * KERNEL)
    half = in_dim // 2
    flipped = weight_full.reshape(KERNEL, KERNEL, in_dim, gate_dim)[::-1, ::-1]
    flipped = flipped.transpose(0, 1, 3, 2).reshape(KERNEL * KERNEL * gate_dim, in_dim)
    grad_weight = jnp.zeros(weight_full.shape, jnp.float32)
    grad_gain = jnp.zeros(gain.shape, jnp.float32)
    grad_shift = jnp.zeros(shift.shape, jnp.float32)
    grad_hidden = jnp.zeros(pixel_shape[:3] + (half,), jnp.float32)
    grad_cells = jnp.zeros(pixel_shape[:3] + (half,), jnp.float32)
    grad_inputs = [None] * len(kept)
    for frame_no in reversed(range(len(kept))):
        padded, gates, cells_prev = kept[frame_no]
        unused, pull = jax.vjp(lstm_cell, gates, cells_prev, gain, shift)
        grad_gates, grad_cells, part_gain, part_shift = pull(
            (grad_above[frame_no] + grad_hidden, grad_cells)
        )
        grad_gain = grad_gain + part_gain
        grad_shift = grad_shift + part_shift
        gates_low = grad_gates.astype(jnp.bfloat16)
        grad_weight = grad_weight + lax.dot_general(
            unfold(padded, rows, columns),
            gates_low.reshape(-1, gate_dim),
            (((0,), (0,)), ((), ())),
            preferred_element_type=jnp.float32,
        )
        spread = padded_2(gates_low, (("tile", 1),), KERNEL // 2)
        spread = pad_columns(spread)
        grad_joined = jnp.dot(
            unfold(spread, rows, columns), flipped, preferred_element_type=jnp.float32
        )
        grad_joined = grad_joined.reshape(pixel_shape[:3] + (in_dim,))
        grad_inputs[frame_no] = grad_joined[..., :half]
        grad_hidden = grad_joined[..., half:]
    return (grad_weight, grad_gain, grad_shift, grad_inputs)


def adamw(weight, moment, second, grad, rate, correction):
    moment_new = 0.5 * moment + 0.5 * grad
    second_new = 0.5 * second + 0.5 * grad * grad
    update = moment_new / correction / (jnp.sqrt(second_new / correction) + 1e-08)
    return (weight - rate * (update + 0.01 * weight), moment_new, second_new)


def per_device(
    observed,
    targets,
    pixel_mask,
    lengths,
    step_count,
    kernels,
    kernel_moment,
    kernel_second,
    norm_params,
    norm_moment,
    norm_second,
    end_params,
    end_moment,
    end_second,
    head_bias,
    head_moment,
    head_second,
    hidden_init,
    cells_init,
):
    frame_total = observed.shape[1]
    layers = kernels.shape[0]
    frame_ids = lax.broadcasted_iota(jnp.int32, (1, frame_total), 1)
    counted = (frame_ids < lengths[:, None]).astype(jnp.float32)
    valid = pixel_mask.astype(jnp.float32) * counted[:, :, None, None]
    count = jnp.maximum(lax.psum(jnp.sum(valid), ("tile", "dp")), 1.0)
    inputs_low = [
        (end_params[0] * observed[:, frame_no, :, :, None] + end_params[1]).astype(jnp.bfloat16)
        for frame_no in range(frame_total)
    ]
    outputs = []
    layer_no = 0
    weight_full = lax.all_gather(kernels[layer_no].astype(jnp.bfloat16), "dp", axis=0, tiled=True)
    outputs, outputs_low, kept, hidden, cells = layer_forward(
        weight_full,
        norm_params[0, layer_no],
        norm_params[1, layer_no],
        inputs_low,
        hidden_init[layer_no],
        cells_init[layer_no],
    )
    stored_kept = [kept]
    hidden_list = [hidden]
    cells_list = [cells]
    loss_sum = jnp.zeros((), jnp.float32)
    grad_head_weight = jnp.zeros(end_params.shape[1:], jnp.float32)
    grad_head = jnp.zeros((1,), jnp.float32)
    grad_above = []
    for frame_no in range(frame_total):
        predicted = jnp.sum(outputs[frame_no] * end_params[2], axis=-1) + head_bias[0]
        error = predicted - targets[:, frame_no]
        weighted = valid[:, frame_no] * error
        loss_sum = loss_sum + jnp.sum(weighted * error)
        grad_pred = 2.0 * weighted / count
        grad_head = grad_head + jnp.sum(grad_pred)
        grad_head_weight = grad_head_weight + jnp.sum(
            grad_pred[..., None] * outputs[frame_no], axis=(0, 1, 2)
        )
        grad_above.append(grad_pred[..., None] * end_params[2])
    kernel_grads = [None] * layers
    gain_grads = [None] * layers
    shift_grads = [None] * layers
    for layer_no in reversed(range(layers)):
        weight_full = lax.all_gather(
            kernels[layer_no].astype(jnp.bfloat16), "dp", axis=0, tiled=True
        )
        grad_weight, grad_gain, grad_shift, grad_inputs = layer_backward(
            weight_full,
            norm_params[0, layer_no],
            norm_params[1, layer_no],
            stored_kept[layer_no],
            grad_above,
        )
        kernel_grads[layer_no] = grad_weight
        gain_grads[layer_no] = grad_gain
        shift_grads[layer_no] = grad_shift
        grad_above = grad_inputs
    grad_lift_weight = jnp.zeros(end_params.shape[1:], jnp.float32)
    grad_lift_bias = jnp.zeros(end_params.shape[1:], jnp.float32)
    for frame_no in range(frame_total):
        grad_lift_weight = grad_lift_weight + jnp.sum(
            grad_above[frame_no] * observed[:, frame_no, :, :, None], axis=(0, 1, 2)
        )
        grad_lift_bias = grad_lift_bias + jnp.sum(grad_above[frame_no], axis=(0, 1, 2))
    grad_norms = jnp.stack([jnp.stack(gain_grads), jnp.stack(shift_grads)])
    grad_ends = jnp.stack([grad_lift_weight, grad_lift_bias, grad_head_weight])
    grad_kernels = jnp.stack(kernel_grads)
    shard = lax.psum_scatter(grad_kernels, "dp", scatter_dimension=1, tiled=True)
    shard = lax.psum(shard, "tile")
    local_square = jnp.sum(shard * shard)
    grad_norms, grad_ends, grad_head, loss_sum = lax.psum(
        (grad_norms, grad_ends, grad_head, loss_sum), ("tile", "dp")
    )
    kernel_square = lax.psum(local_square, "dp")
    squares = (
        kernel_square
        + jnp.sum(grad_norms * grad_norms)
        + jnp.sum(grad_ends * grad_ends)
        + jnp.sum(grad_head * grad_head)
    )
    grad_norm = jnp.sqrt(squares)
    factor = clip_limit / jnp.maximum(grad_norm, clip_limit)
    correction = 1.0 - jnp.power(0.5, step_count[0].astype(jnp.float32))
    kernel_rate = (KERNEL * KERNEL * IN_DIM) ** (-0.5)
    kern_out = adamw(kernels, kernel_moment, kernel_second, shard * factor, kernel_rate, correction)
    norm_out = adamw(
        norm_params, norm_moment, norm_second, grad_norms * factor, small_rate, correction
    )
    end_out = adamw(end_params, end_moment, end_second, grad_ends * factor, small_rate, correction)
    head_out = adamw(
        head_bias, head_moment, head_second, grad_head * factor, small_rate, correction
    )
    loss_value = loss_sum / count
    return (
        loss_value,
        grad_norm,
        kern_out[0],
        kern_out[1],
        kern_out[2],
        norm_out[0],
        norm_out[1],
        norm_out[2],
        end_out[0],
        end_out[1],
        end_out[2],
        head_out[0],
        head_out[1],
        head_out[2],
        jnp.stack(hidden_list),
        jnp.stack(cells_list),
    )


def solution(mesh):
    placed = (
        P("dp", None, "tile", None),
        P("dp", None, "tile", None),
        P("dp", None, "tile", None),
        P("dp"),
        P(),
        P(None, "dp", None),
        P(None, "dp", None),
        P(None, "dp", None),
        P(),
        P(),
        P(),
        P(),
        P(),
        P(),
        P(),
        P(),
        P(),
        P(None, "dp", "tile", None, None),
        P(None, "dp", "tile", None, None),
    )
    return jax.shard_map(
        per_device,
        mesh=mesh,
        in_specs=placed,
        out_specs=(
            P(),
            P(),
            P(None, "dp", None),
            P(None, "dp", None),
            P(None, "dp", None),
            P(),
            P(),
            P(),
            P(),
            P(),
            P(),
            P(),
            P(),
            P(),
            P(None, "dp", "tile", None, None),
            P(None, "dp", "tile", None, None),
        ),
        check_vma=False,
    )
```

profile of v0, /device:TPU:0, one launch (start us, length us, event | category | flops | bytes accessed | tf_op | source)
XLA Modules:
  0.0 1688.5 jit_solution(5633768059832277343)
XLA Ops:
  7.2 5.1 convert_element_type.95
  13.2 1.3 collective-permute-start.1
  14.5 3.0 collective-permute-start
  18.9 85.6 %psum.50 = f32[]{:T(128)} all-reduce(f32[]{:T(128)} %get-tuple-element.65), channel_id=1, replica_groups=mesh['tile'=4,'dp'=8] {'tile','dp'}, use_global_device_ids=true, to_apply=%region_10.11 | all-reduce | flops 1 | bytes 8 | tf_op jit(solution)/shard_map/psum | solution.py:159
  108.5 408.1 %all-gather.3.cloned.1.call-done = bf16[1,12800,1024]{2,1,0:T(8,128)(2,1)} async-done(((bf16[1,1600,1024]{2,1,0:T(8,128)(2,1)}), bf16[1,12800,1024]{2,1,0:T(8,128)(2,1)}) %all-gather.3.cloned.1.call-update) | async-done | bytes 26214416 | tf_op jit(solution)/shard_map/all_gather | solution.py:166
  516.7 10.8 fusion.3
  530.1 1.3 collective-permute-start.3
  531.4 3.0 collective-permute-start.2
  534.4 18.4 %reverse_bitcast_fusion = bf16[5,5,1024,512]{2,3,1,0:T(8,128)(2,1)} fusion(bf16[5,5,512,1024]{3,2,1,0:T(8,128)(2,1)} %bitcast.214), kind=kLoop, calls=%fused_computation.6 | loop fusion | bytes 52428800 | tf_op jit(solution)/shard_map/transpose | solution.py:93
  552.8 33.9 %copy.35 = bf16[5,5,1024,512]{3,2,1,0:T(8,128)(2,1)} copy(bf16[5,5,1024,512]{2,3,1,0:T(8,128)(2,1)} %reverse_bitcast_fusion) | data formatting | bytes 52428800 | tf_op jit(solution)/shard_map/transpose | solution.py:93
  588.8 10.8 fusion.1
  606.1 1.3 collective-permute-start.5
  607.4 3.8 collective-permute-start.4
  611.2 21.6 %fusion.11 = f32[12800,1024,1]{1,0,2:T(8,128)} fusion(bf16[1,2,32,12800]{3,2,1,0:T(8,128)(2,1)} %copy-done, bf16[1,2,32,1024]{3,2,1,0:T(8,128)(2,1)S(1)} %fusion.25), kind=kOutput, calls=%fused_computation.17 | convolution fusion | flops 1677721600 | bytes 54198272 | tf_op jit(solution)/shard_map/dot_general | solution.py:109
  633.8 10.8 fusion.13
  647.9 33.5 %fusion = f32[1,12800,1024]{2,1,0:T(8,128)} fusion(f32[12800,1024,1]{1,0,2:T(8,128)} %fusion.11, bf16[1,2,32,12800]{3,2,1,0:T(8,128)(2,1)S(1)} %copy-done.2, bf16[1,2,32,1024]{3,2,1,0:T(8,128)(2,1)S(1)} %fusion.27), kind=kOutput, calls=%fused_computation.1 | convolution fusion | flops 1690828800 | bytes 106627072 | tf_op jit(solution)/shard_map/dot_general | solution.py:109
  684.8 4.5 collective-permute-start.6
  705.7 793.9 %reduce-scatter.2.cloned.1.call-done = f32[1,1600,1024]{2,1,0:T(8,128)} async-done(((f32[1,12800,1024]{2,1,0:T(8,128)}), f32[1,1600,1024]{2,1,0:T(8,128)}) %reduce-scatter.2.cloned.1.call-update) | async-done | bytes 6553616 | tf_op jit(solution)/shard_map/reduce_scatter | solution.py:221
  1503.7 12.9 fusion.16
  1516.8 41.4 %all-reduce.12 = (f32[]{:T(128)}, f32[2,1,1024]{2,1,0:T(1,128)S(1)}, f32[3,256]{1,0:T(4,128)S(1)}, f32[1]{0:T(128)}) all-reduce(f32[]{:T(128)S(6)} %add.410, f32[2,1,1024]{2,1,0:T(1,128)S(1)} %pad_maximum_fusion.14, f32[3,256]{1,0:T(4,128)S(1)} %pad_maximum_fusion.15, f32[1]{0:T(128)} %bitcast.95), channel_id=1, replica_groups=mesh['tile'=4,'dp'=8] {'tile','dp'}, use_global_device_ids=true, to_apply=%region_8.9 | all-reduce | flops 2818 | bytes 22544 | tf_op jit(solution)/shard_map/psum | solution.py:224
  1560.1 66.4 %all-reduce.15.cloned.1.call-done = f32[1,1600,1024]{2,1,0:T(8,128)} async-done(((f32[1,1600,1024]{2,1,0:T(8,128)}), f32[1,1600,1024]{2,1,0:T(8,128)}) %all-reduce.15.cloned.1.call-update) | async-done | bytes 6553616 | tf_op jit(solution)/shard_map/psum | solution.py:222
  1626.4 5.1 multiply_reduce_fusion
  1632.9 22.0 %psum.52 = f32[]{:T(128)} all-reduce(f32[]{:T(128)} %multiply_reduce_fusion), channel_id=1, replica_groups=mesh['tile'=4,'dp'=8] {'dp'}, use_global_device_ids=true, to_apply=%region_18.19 | all-reduce | flops 1 | bytes 8 | tf_op jit(solution)/shard_map/psum | solution.py:227
  1659.0 17.3 %multiply_subtract_fusion = (f32[1,1600,1024]{2,1,0:T(8,128)}, f32[1,1600,1024]{2,1,0:T(8,128)}, f32[1,1600,1024]{2,1,0:T(8,128)}) fusion(f32[1,1600,1024]{2,1,0:T(8,128)} %param.24, f32[]{:T(128)} %bitcast.97, f32[1,1600,1024]{2,1,0:T(8,128)} %all-reduce.15.cloned.1.call-done, f32[]{:T(128)} %div.177, f32[1,1600,1024]{2,1,0:T(8,128)} %param.26, ...), kind=kLoop, calls=%fused_computation.10 | loop fusion | flops 24576000 | bytes 45875208 | tf_op jit(solution)/shard_map/sub | solution.py:130
  (289 shorter events, 40.2 us)
Async XLA Ops:
  7.2 509.5 %all-gather.3.cloned.1.call-start = ((), (), s32[]{:S(2)}) async-start(), calls=%async_computation.3 | async-start | bytes 29491200 | tf_op jit(solution)/shard_map/all_gather | solution.py:166
  12.3 5.9 copy-start.7
  12.3 5.9 copy-start.19
  12.4 1487.3 %reduce-scatter.2.cloned.1.call-start = ((), (), s32[]{:S(2)}) async-start(), calls=%async_computation.1 | async-start | bytes 58982400 | tf_op jit(solution)/shard_map/reduce_scatter | solution.py:221
  13.0 93.6 %copy-start.9 = (f32[2,32]{1,0:T(2,128)}, f32[2,32]{1,0:T(2,128)S(1)}, u32[]{:S(2)}) copy-start(f32[2,32]{1,0:T(2,128)S(1)} %get-tuple-element.135) | copy-start | bytes 772
  13.2 92.8 %collective-permute-start.1 = (bf16[1,2,32,512]{3,2,1,0:T(8,128)(2,1)S(1)}, bf16[1,2,32,512]{3,2,1,0:T(8,128)(2,1)S(1)}, u32[]{:S(2)}, u32[]{:S(2)}) collective-permute-start(bf16[1,2,32,512]{3,2,1,0:T(8,128)(2,1)S(1)} %pad_maximum_fusion.12), channel_id=1, source_target_pairs={{8,0},{16,8},{24,16},{9,1},{17,9},{25,17},{10,2},{18,10},{26,18},{... | collective-permute-start | bytes 196616 | tf_op jit(solution)/shard_map/ppermute | solution.py:23
  14.5 91.5 %collective-permute-start = (bf16[1,2,32,512]{3,2,1,0:T(8,128)(2,1)S(1)}, bf16[1,2,32,512]{3,2,1,0:T(8,128)(2,1)S(1)}, u32[]{:S(2)}, u32[]{:S(2)}) collective-permute-start(bf16[1,2,32,512]{3,2,1,0:T(8,128)(2,1)S(1)} %pad_maximum_fusion.12), channel_id=1, source_target_pairs={{0,8},{8,16},{16,24},{1,9},{9,17},{17,25},{2,10},{10,18},{18,26},{... | collective-permute-start | bytes 196616 | tf_op jit(solution)/shard_map/ppermute | solution.py:21
  530.1 56.6 %collective-permute-start.3 = (bf16[1,2,32,512]{3,2,1,0:T(8,128)(2,1)S(1)}, bf16[1,2,32,512]{3,2,1,0:T(8,128)(2,1)S(1)}, u32[]{:S(2)}, u32[]{:S(2)}) collective-permute-start(bf16[1,2,32,512]{3,2,1,0:T(8,128)(2,1)S(1)} %pad_maximum_fusion.13), channel_id=1, source_target_pairs={{8,0},{16,8},{24,16},{9,1},{17,9},{25,17},{10,2},{18,10},{26,18},{... | collective-permute-start | bytes 196616 | tf_op jit(solution)/shard_map/ppermute | solution.py:23
  531.4 55.3 %collective-permute-start.2 = (bf16[1,2,32,512]{3,2,1,0:T(8,128)(2,1)S(1)}, bf16[1,2,32,512]{3,2,1,0:T(8,128)(2,1)S(1)}, u32[]{:S(2)}, u32[]{:S(2)}) collective-permute-start(bf16[1,2,32,512]{3,2,1,0:T(8,128)(2,1)S(1)} %pad_maximum_fusion.13), channel_id=1, source_target_pairs={{0,8},{8,16},{16,24},{1,9},{9,17},{17,25},{2,10},{10,18},{18,26},{... | collective-permute-start | bytes 196616 | tf_op jit(solution)/shard_map/ppermute | solution.py:21
  601.1 1.8 copy-start.15
  602.8 41.9 %copy-start.3 = (f32[1,2,32,256]{3,2,1,0:T(8,128)}, f32[1,2,32,256]{3,2,1,0:T(8,128)S(1)}, u32[]{:S(2)}) copy-start(f32[1,2,32,256]{3,2,1,0:T(8,128)S(1)} %get-tuple-element.37) | copy-start | bytes 196612
  606.1 26.7 %collective-permute-start.5 = (bf16[1,2,32,1024]{3,2,1,0:T(8,128)(2,1)S(1)}, bf16[1,2,32,1024]{3,2,1,0:T(8,128)(2,1)S(1)}, u32[]{:S(2)}, u32[]{:S(2)}) collective-permute-start(bf16[1,2,32,1024]{3,2,1,0:T(8,128)(2,1)S(1)} %fusion.25), channel_id=1, source_target_pairs={{8,0},{16,8},{24,16},{9,1},{17,9},{25,17},{10,2},{18,10},{26,18},{... | collective-permute-start | bytes 393224 | tf_op jit(solution)/shard_map/ppermute | solution.py:23
  607.4 25.4 %collective-permute-start.4 = (bf16[1,2,32,1024]{3,2,1,0:T(8,128)(2,1)S(1)}, bf16[1,2,32,1024]{3,2,1,0:T(8,128)(2,1)S(1)}, u32[]{:S(2)}, u32[]{:S(2)}) collective-permute-start(bf16[1,2,32,1024]{3,2,1,0:T(8,128)(2,1)S(1)} %fusion.25), channel_id=1, source_target_pairs={{0,8},{8,16},{16,24},{1,9},{9,17},{17,25},{2,10},{10,18},{18,26},{... | collective-permute-start | bytes 393224 | tf_op jit(solution)/shard_map/ppermute | solution.py:21
  633.8 11.0 copy-start.6
  681.5 944.9 %all-reduce.15.cloned.1.call-start = ((), (), s32[]{:S(2)}) async-start(), calls=%async_computation.2 | async-start | bytes 13107200 | tf_op jit(solution)/shard_map/psum | solution.py:222
  683.5 9.1 collective-permute-start.7
  684.8 7.8 collective-permute-start.6
  1503.7 12.9 copy-start.10
  1560.0 97.7 %copy-start.8 = (f32[2,1,1024]{2,1,0:T(1,128)S(1)}, f32[2,1,1024]{2,1,0:T(1,128)}, u32[]{:S(2)}) copy-start(f32[2,1,1024]{2,1,0:T(1,128)} %param.27) | copy-start | bytes 24580
  1560.0 97.7 %copy-start.13 = (f32[2,1,1024]{2,1,0:T(1,128)S(1)}, f32[2,1,1024]{2,1,0:T(1,128)}, u32[]{:S(2)}) copy-start(f32[2,1,1024]{2,1,0:T(1,128)} %param.29) | copy-start | bytes 24580
  1560.0 97.7 %copy-start.14 = (f32[2,1,1024]{2,1,0:T(1,128)S(1)}, f32[2,1,1024]{2,1,0:T(1,128)}, u32[]{:S(2)}) copy-start(f32[2,1,1024]{2,1,0:T(1,128)} %param.28) | copy-start | bytes 24580
  1560.0 98.3 %copy-start.12 = (f32[3,256]{1,0:T(4,128)S(1)}, f32[3,256]{1,0:T(4,128)}, u32[]{:S(2)}) copy-start(f32[3,256]{1,0:T(4,128)} %param.30) | copy-start | bytes 9220
  1560.0 98.3 %copy-start.16 = (f32[3,256]{1,0:T(4,128)S(1)}, f32[3,256]{1,0:T(4,128)}, u32[]{:S(2)}) copy-start(f32[3,256]{1,0:T(4,128)} %param.32) | copy-start | bytes 9220
  1560.0 98.3 %copy-start.17 = (f32[3,256]{1,0:T(4,128)S(1)}, f32[3,256]{1,0:T(4,128)}, u32[]{:S(2)}) copy-start(f32[3,256]{1,0:T(4,128)} %param.31) | copy-start | bytes 9220
  (7 other events, 7.4 us)
Sparse Core Ops, SparseCore 0:
  12.5 504.1 all-gather.2
  681.6 817.9 reduce-scatter.1
  1502.0 124.3 all-reduce.14
where the time goes:
time: 1690 us
  waiting for transfers between devices  1270 us (75%)
  blocking collectives  149 us (9%)
  matrix products  100 us (6%)
  local copies, waits for them, and re-layouts  76.5 us (5%)
  other arithmetic  41.9 us (2%)
  between operations  32.4 us (2%)
  starting transfers between devices  19.7 us (1%)
    reduce_scatter x1, waiting for transfers between devices, per_device(): lax.psum_scatter(grad_kernels, 'dp', scatter_dimension=1, tiled=True)  794 us
    all_gather x1, waiting for transfers between devices, per_device(): lax.all_gather(kernels[layer_no].astype(jnp.bfloat16), 'dp', axis=0, tile...  408 us
    psum x1, blocking collectives, per_device(): count = jnp.maximum(lax.psum(jnp.sum(valid), ('tile', 'dp')), 1.0)  85.6 us
    psum x1, waiting for transfers between devices, per_device(): shard = lax.psum(shard, 'tile')  66.4 us
    dot_general x2, matrix products, layer_backward(): lax.dot_general(unfold(padded, rows, columns), gates_low.reshape(-1, gate...  55.1 us
    transpose x2, local copies, waits for them, and re-layouts, layer_backward(): flipped.transpose(0, 1, 3, 2).reshape(KERNEL * KERNEL * gate_dim, in_dim)  52.3 us
    psum x1, blocking collectives, per_device(): lax.psum((grad_norms, grad_ends, grad_head, loss_sum), ('tile', 'dp'))  41.4 us
  transfers between devices with their start and end apart: 11, of which 3 were waited for; matrix products, arithmetic and copies ran while one was open for 6% of the time, Pallas kernels for 0%

commit v1 on v0

--- a/solution.py
+++ b/solution.py
@@ -2,12 +2,22 @@
 import jax.numpy as jnp
 from jax import lax
 from jax.sharding import PartitionSpec as P
+from jax.lax import axis_size, ppermute
 
 IN_DIM = 512
 KERNEL = 5
 GROUP_SIZE = 64
 clip_limit = 0.005
 small_rate = 0.1
+
+
+def guide_hubs(frame_in):
+    n_axis = axis_size("tile")
+    tile_out = frame_in
+    for j0 in [num for num in (1, 2, 4, 8, 16) if num < n_axis]:
+        d_next = ppermute(tile_out, "tile", [(m, m ^ j0) for m in range(n_axis)])
+        tile_out = tile_out + d_next
+    return tile_out
 
 
 def padded_2(cells, sides, width):
@@ -219,7 +229,7 @@
     grad_ends = jnp.stack([grad_lift_weight, grad_lift_bias, grad_head_weight])
     grad_kernels = jnp.stack(kernel_grads)
     shard = lax.psum_scatter(grad_kernels, "dp", scatter_dimension=1, tiled=True)
-    shard = lax.psum(shard, "tile")
+    shard = guide_hubs(shard)
     local_square = jnp.sum(shard * shard)
     grad_norms, grad_ends, grad_head, loss_sum = lax.psum(
         (grad_norms, grad_ends, grad_head, loss_sum), ("tile", "dp")

time: 1690 us -> 1770 us (1.047)
  blocking collectives: 149 us -> 271 us
  waiting for transfers between devices: 1270 us -> 1230 us
    psum x1, blocking collectives: 41.4 us -> 163 us  [per_device(): lax.psum((grad_norms, grad_ends, grad_head, loss_sum), ('tile', 'dp'))]
    psum x1 -> x0, waiting for transfers between devices: 66.4 us -> none  [per_device(): shard = lax.psum(shard, 'tile')]
    reduce_scatter x1, waiting for transfers between devices: 794 us -> 818 us  [per_device(): lax.psum_scatter(grad_kernels, 'dp', scatter_dimension=1, tiled=True)]
  transfers between devices with their start and end apart: 11 -> 12, of which waited for: 3 -> 3; matrix products, arithmetic and copies ran while one was open for 6% -> 5% of each run, Pallas kernels for 0% -> 0%
where the time goes in v1:
time: 1770 us
  waiting for transfers between devices  1230 us (69%)
  blocking collectives  271 us (15%)
  matrix products  98.3 us (6%)
  local copies, waits for them, and re-layouts  61.5 us (3%)
  other arithmetic  57.2 us (3%)
  between operations  32.9 us (2%)
  starting transfers between devices  19.9 us (1%)
    reduce_scatter x1, waiting for transfers between devices, per_device(): lax.psum_scatter(grad_kernels, 'dp', scatter_dimension=1, tiled=True)  818 us
    all_gather x1, waiting for transfers between devices, per_device(): lax.all_gather(kernels[layer_no].astype(jnp.bfloat16), 'dp', axis=0, tile...  408 us
    psum x1, blocking collectives, per_device(): lax.psum((grad_norms, grad_ends, grad_head, loss_sum), ('tile', 'dp'))  163 us
    psum x1, blocking collectives, per_device(): count = jnp.maximum(lax.psum(jnp.sum(valid), ('tile', 'dp')), 1.0)  85.6 us
    dot_general x2, matrix products, layer_backward(): lax.dot_general(unfold(padded, rows, columns), gates_low.reshape(-1, gate...  55.1 us
    transpose x2, local copies, waits for them, and re-layouts, layer_backward(): flipped.transpose(0, 1, 3, 2).reshape(KERNEL * KERNEL * gate_dim, in_dim)  52.3 us
  transfers between devices with their start and end apart: 12, of which 3 were waited for; matrix products, arithmetic and copies ran while one was open for 5% of the time, Pallas kernels for 0%

profile of v1, /device:TPU:0, one launch (start us, length us, event | category | flops | bytes accessed | tf_op | source)
XLA Modules:
  0.0 1767.7 jit_solution(3304890145225893677)
XLA Ops:
  7.2 5.1 convert_element_type.95
  13.2 1.3 collective-permute-start.1
  14.5 3.0 collective-permute-start
  18.9 85.6 %psum.43 = f32[]{:T(128)} all-reduce(f32[]{:T(128)} %get-tuple-element.67), channel_id=1, replica_groups=mesh['tile'=4,'dp'=8] {'tile','dp'}, use_global_device_ids=true, to_apply=%region_10.11 | all-reduce | flops 1 | bytes 8 | tf_op jit(solution)/shard_map/psum | solution.py:169
  108.5 408.1 %all-gather.3.cloned.1.call-done = bf16[1,12800,1024]{2,1,0:T(8,128)(2,1)} async-done(((bf16[1,1600,1024]{2,1,0:T(8,128)(2,1)}), bf16[1,12800,1024]{2,1,0:T(8,128)(2,1)}) %all-gather.3.cloned.1.call-update) | async-done | bytes 26214416 | tf_op jit(solution)/shard_map/all_gather | solution.py:176
  516.7 10.8 fusion.3
  530.1 1.3 collective-permute-start.3
  531.4 3.0 collective-permute-start.2
  534.4 18.4 %reverse_bitcast_fusion = bf16[5,5,1024,512]{2,3,1,0:T(8,128)(2,1)} fusion(bf16[5,5,512,1024]{3,2,1,0:T(8,128)(2,1)} %bitcast.214), kind=kLoop, calls=%fused_computation.6 | loop fusion | bytes 52428800 | tf_op jit(solution)/shard_map/transpose | solution.py:103
  552.8 33.9 %copy.35 = bf16[5,5,1024,512]{3,2,1,0:T(8,128)(2,1)} copy(bf16[5,5,1024,512]{2,3,1,0:T(8,128)(2,1)} %reverse_bitcast_fusion) | data formatting | bytes 52428800 | tf_op jit(solution)/shard_map/transpose | solution.py:103
  588.8 10.8 fusion.1
  607.9 3.8 collective-permute-start.4
  611.7 21.6 %fusion.11 = f32[12800,1024,1]{1,0,2:T(8,128)} fusion(bf16[1,2,32,12800]{3,2,1,0:T(8,128)(2,1)} %copy-done, bf16[1,2,32,1024]{3,2,1,0:T(8,128)(2,1)S(1)} %fusion.25), kind=kOutput, calls=%fused_computation.17 | convolution fusion | flops 1677721600 | bytes 54198272 | tf_op jit(solution)/shard_map/dot_general | solution.py:119
  634.4 10.8 fusion.13
  649.1 33.5 %fusion = f32[1,12800,1024]{2,1,0:T(8,128)} fusion(f32[12800,1024,1]{1,0,2:T(8,128)} %fusion.11, bf16[1,2,32,12800]{3,2,1,0:T(8,128)(2,1)S(1)} %copy-done.2, bf16[1,2,32,1024]{3,2,1,0:T(8,128)(2,1)S(1)} %fusion.27), kind=kOutput, calls=%fused_computation.1 | convolution fusion | flops 1690828800 | bytes 106627072 | tf_op jit(solution)/shard_map/dot_general | solution.py:119
  682.6 818.0 %reduce-scatter.2.cloned.1.call-done = f32[1,1600,1024]{2,1,0:T(8,128)} async-done(((f32[1,12800,1024]{2,1,0:T(8,128)}), f32[1,1600,1024]{2,1,0:T(8,128)}) %reduce-scatter.2.cloned.1.call-update) | async-done | bytes 6553616 | tf_op jit(solution)/shard_map/reduce_scatter | solution.py:231
  1504.0 3.3 collective-permute-start.8
  1511.8 9.9 add.421
  1521.7 1.5 collective-permute-start.7
  1524.0 10.7 fusion.16
  1534.9 163.3 %all-reduce.12 = (f32[]{:T(128)}, f32[2,1,1024]{2,1,0:T(1,128)S(1)}, f32[3,256]{1,0:T(4,128)S(1)}, f32[1]{0:T(128)}) all-reduce(f32[]{:T(128)S(6)} %add.414, f32[2,1,1024]{2,1,0:T(1,128)S(1)} %pad_maximum_fusion.14, f32[3,256]{1,0:T(4,128)S(1)} %pad_maximum_fusion.15, f32[1]{0:T(128)} %bitcast.95), channel_id=1, replica_groups=mesh['tile'=4,'dp'=8] {'tile','dp'}, use_global_device_ids=true, to_apply=%region_8.9 | all-reduce | flops 2818 | bytes 22544 | tf_op jit(solution)/shard_map/psum | solution.py:234
  1701.4 10.7 multiply_reduce_fusion
  1712.0 21.7 %psum.44 = f32[]{:T(128)} all-reduce(f32[]{:T(128)} %get-tuple-element.47), channel_id=1, replica_groups=mesh['tile'=4,'dp'=8] {'dp'}, use_global_device_ids=true, to_apply=%region_17.18 | all-reduce | flops 1 | bytes 8 | tf_op jit(solution)/shard_map/psum | solution.py:237
  1737.9 17.3 multiply_subtract_fusion
  (297 shorter events, 27.3 us)
Async XLA Ops:
  7.2 509.5 %all-gather.3.cloned.1.call-start = ((), (), s32[]{:S(2)}) async-start(), calls=%async_computation.2 | async-start | bytes 29491200 | tf_op jit(solution)/shard_map/all_gather | solution.py:176
  12.4 1488.3 %reduce-scatter.2.cloned.1.call-start = ((), (), s32[]{:S(2)}) async-start(), calls=%async_computation.1 | async-start | bytes 58982400 | tf_op jit(solution)/shard_map/reduce_scatter | solution.py:231
  13.0 93.6 %copy-start.9 = (f32[2,32]{1,0:T(2,128)}, f32[2,32]{1,0:T(2,128)S(1)}, u32[]{:S(2)}) copy-start(f32[2,32]{1,0:T(2,128)S(1)} %get-tuple-element.137) | copy-start | bytes 772
  13.2 92.8 %collective-permute-start.1 = (bf16[1,2,32,512]{3,2,1,0:T(8,128)(2,1)S(1)}, bf16[1,2,32,512]{3,2,1,0:T(8,128)(2,1)S(1)}, u32[]{:S(2)}, u32[]{:S(2)}) collective-permute-start(bf16[1,2,32,512]{3,2,1,0:T(8,128)(2,1)S(1)} %pad_maximum_fusion.12), channel_id=1, source_target_pairs={{8,0},{16,8},{24,16},{9,1},{17,9},{25,17},{10,2},{18,10},{26,18},{... | collective-permute-start | bytes 196616 | tf_op jit(solution)/shard_map/ppermute | solution.py:33
  14.5 91.5 %collective-permute-start = (bf16[1,2,32,512]{3,2,1,0:T(8,128)(2,1)S(1)}, bf16[1,2,32,512]{3,2,1,0:T(8,128)(2,1)S(1)}, u32[]{:S(2)}, u32[]{:S(2)}) collective-permute-start(bf16[1,2,32,512]{3,2,1,0:T(8,128)(2,1)S(1)} %pad_maximum_fusion.12), channel_id=1, source_target_pairs={{0,8},{8,16},{16,24},{1,9},{9,17},{17,25},{2,10},{10,18},{18,26},{... | collective-permute-start | bytes 196616 | tf_op jit(solution)/shard_map/ppermute | solution.py:31
  530.1 56.6 %collective-permute-start.3 = (bf16[1,2,32,512]{3,2,1,0:T(8,128)(2,1)S(1)}, bf16[1,2,32,512]{3,2,1,0:T(8,128)(2,1)S(1)}, u32[]{:S(2)}, u32[]{:S(2)}) collective-permute-start(bf16[1,2,32,512]{3,2,1,0:T(8,128)(2,1)S(1)} %pad_maximum_fusion.13), channel_id=1, source_target_pairs={{8,0},{16,8},{24,16},{9,1},{17,9},{25,17},{10,2},{18,10},{26,18},{... | collective-permute-start | bytes 196616 | tf_op jit(solution)/shard_map/ppermute | solution.py:33
  531.4 55.3 %collective-permute-start.2 = (bf16[1,2,32,512]{3,2,1,0:T(8,128)(2,1)S(1)}, bf16[1,2,32,512]{3,2,1,0:T(8,128)(2,1)S(1)}, u32[]{:S(2)}, u32[]{:S(2)}) collective-permute-start(bf16[1,2,32,512]{3,2,1,0:T(8,128)(2,1)S(1)} %pad_maximum_fusion.13), channel_id=1, source_target_pairs={{0,8},{8,16},{16,24},{1,9},{9,17},{17,25},{2,10},{10,18},{18,26},{... | collective-permute-start | bytes 196616 | tf_op jit(solution)/shard_map/ppermute | solution.py:31
  602.8 42.4 %copy-start.3 = (f32[1,2,32,256]{3,2,1,0:T(8,128)}, f32[1,2,32,256]{3,2,1,0:T(8,128)S(1)}, u32[]{:S(2)}) copy-start(f32[1,2,32,256]{3,2,1,0:T(8,128)S(1)} %get-tuple-element.37) | copy-start | bytes 196612
  606.6 26.7 %collective-permute-start.5 = (bf16[1,2,32,1024]{3,2,1,0:T(8,128)(2,1)S(1)}, bf16[1,2,32,1024]{3,2,1,0:T(8,128)(2,1)S(1)}, u32[]{:S(2)}, u32[]{:S(2)}) collective-permute-start(bf16[1,2,32,1024]{3,2,1,0:T(8,128)(2,1)S(1)} %fusion.25), channel_id=1, source_target_pairs={{8,0},{16,8},{24,16},{9,1},{17,9},{25,17},{10,2},{18,10},{26,18},{... | collective-permute-start | bytes 393224 | tf_op jit(solution)/shard_map/ppermute | solution.py:33
  607.9 25.4 %collective-permute-start.4 = (bf16[1,2,32,1024]{3,2,1,0:T(8,128)(2,1)S(1)}, bf16[1,2,32,1024]{3,2,1,0:T(8,128)(2,1)S(1)}, u32[]{:S(2)}, u32[]{:S(2)}) collective-permute-start(bf16[1,2,32,1024]{3,2,1,0:T(8,128)(2,1)S(1)} %fusion.25), channel_id=1, source_target_pairs={{0,8},{8,16},{16,24},{1,9},{9,17},{17,25},{2,10},{10,18},{18,26},{... | collective-permute-start | bytes 393224 | tf_op jit(solution)/shard_map/ppermute | solution.py:31
  634.4 10.9 copy-start.16
  634.4 11.6 copy-start.6
  682.6 827.9 %copy-start.17 = (f32[256]{0:T(256)S(1)}, f32[256]{0:T(256)}, u32[]{:S(2)}) copy-start(f32[256]{0:T(256)} %get-tuple-element.124) | copy-start | bytes 3076
  682.6 827.9 %copy-start.18 = (f32[256]{0:T(256)S(1)}, f32[256]{0:T(256)}, u32[]{:S(2)}) copy-start(f32[256]{0:T(256)} %get-tuple-element.125) | copy-start | bytes 3076
  1500.7 11.2 collective-permute-start.6
  1502.7 8.9 collective-permute-start.9
  1504.0 7.6 collective-permute-start.8
  1521.7 179.6 %collective-permute-start.7 = (f32[1,1600,1024]{2,1,0:T(8,128)}, f32[1,1600,1024]{2,1,0:T(8,128)}, u32[]{:S(2)}, u32[]{:S(2)}) collective-permute-start(f32[1,1600,1024]{2,1,0:T(8,128)} %add.421), channel_id=1, source_target_pairs={{0,16},{8,24},{16,0},{24,8},{1,17},{9,25},{17,1},{25,9},{2,18},{10... | collective-permute-start | bytes 19660808 | tf_op jit(solution)/shard_map/ppermute | solution.py:18
  1701.3 35.3 %copy-start.8 = (f32[2,1,1024]{2,1,0:T(1,128)S(1)}, f32[2,1,1024]{2,1,0:T(1,128)}, u32[]{:S(2)}) copy-start(f32[2,1,1024]{2,1,0:T(1,128)} %param.27) | copy-start | bytes 24580
  1701.3 35.3 %copy-start.13 = (f32[2,1,1024]{2,1,0:T(1,128)S(1)}, f32[2,1,1024]{2,1,0:T(1,128)}, u32[]{:S(2)}) copy-start(f32[2,1,1024]{2,1,0:T(1,128)} %param.29) | copy-start | bytes 24580
  1701.3 35.3 %copy-start.14 = (f32[2,1,1024]{2,1,0:T(1,128)S(1)}, f32[2,1,1024]{2,1,0:T(1,128)}, u32[]{:S(2)}) copy-start(f32[2,1,1024]{2,1,0:T(1,128)} %param.28) | copy-start | bytes 24580
  1701.3 36.0 %copy-start.12 = (f32[3,256]{1,0:T(4,128)S(1)}, f32[3,256]{1,0:T(4,128)}, u32[]{:S(2)}) copy-start(f32[3,256]{1,0:T(4,128)} %param.30) | copy-start | bytes 9220
  1701.3 36.0 %copy-start.19 = (f32[3,256]{1,0:T(4,128)S(1)}, f32[3,256]{1,0:T(4,128)}, u32[]{:S(2)}) copy-start(f32[3,256]{1,0:T(4,128)} %param.32) | copy-start | bytes 9220
  1701.3 36.0 %copy-start.20 = (f32[3,256]{1,0:T(4,128)S(1)}, f32[3,256]{1,0:T(4,128)}, u32[]{:S(2)}) copy-start(f32[3,256]{1,0:T(4,128)} %param.31) | copy-start | bytes 9220
  (11 other events, 31.7 us)
Sparse Core Ops, SparseCore 0:
  12.5 504.1 all-gather.2
  682.7 817.8 reduce-scatter.1
